TPU v7x, 512 devices: a whole 4x8x8 slice. The times are simulated.
512 devices in a mesh: segment: 2 (over core), dp: 64 (over y, z), rows: 4 (over x).
Axes of the slice: x: 4, y: 8, z: 8, core: 2. Of those that a mesh axis runs over, the one named last changes fastest.
Arguments:
- latent: bfloat16 [128, 16, 16, 320], P('dp', 'rows'), may hold values from -6 to 6
- hint: bfloat16 [128, 16, 16, 320], P('dp', 'rows'), may hold values from -6 to 6
- decoder_in: bfloat16 [128, 16, 16, 320], P('dp', 'rows'), may hold values from -6 to 6
- target: bfloat16 [128, 16, 16, 320], P('dp', 'rows'), may hold values from -6 to 6
- first_convs: bfloat16 [2, 2, 2880, 320], P('segment', None, 'dp'), may hold values from -0.109375 to 0.109375
- second_convs: bfloat16 [2, 2880, 320], P('segment', 'dp'), may hold values from -0.109375 to 0.109375
- pointwise_weights: bfloat16 [2, 2, 320, 320], P('segment', None, 'dp'), may hold values from -0.3125 to 0.3125
Outputs:
- grad_first: float32 [921600], P(('segment', 'dp', 'rows'))
- grad_zero: float32 [102400], P(('segment', 'dp', 'rows'))
All inputs are finite; a program needn't handle non-finite values.
Results may differ from a plain program's by a relative error of at most 0.0095.
Values may be sent and summed in bfloat16 or wider, within the bound.
A program may use at most 64 MiB of HBM per device.

v0:
```python
import math
import jax
import jax.numpy as jnp
from jax import lax
from jax.sharding import PartitionSpec as P


def padded_2(block, sides, width):
    for axis, dim in sides:
        count = lax.axis_size(axis)
        forward = [(i, i + 1) for i in range(count - 1)]
        backward = [(target, source) for source, target in forward]
        low = lax.ppermute(
            lax.slice_in_dim(block, block.shape[dim] - width, None, axis=dim), axis, forward
        )
        high = lax.ppermute(lax.slice_in_dim(block, 0, width, axis=dim), axis, backward)
        block = jnp.concatenate([low, block, high], axis=dim)
    return block


def shifted(array, axis, by):
    count = lax.axis_size(axis)
    pairs = [(i, i + by) for i in range(count) if 0 <= i + by < count]
    return lax.ppermute(array, axis, pairs)


def swish_slope(value):
    logistic = jax.nn.sigmoid(value)
    return logistic * (1.0 + value * (1.0 - logistic))


def conv_rows(padded, weight):
    kernel = weight.reshape(3, 3, weight.shape[0] // 9, weight.shape[1])
    return lax.conv_general_dilated(
        padded,
        kernel,
        (1, 1),
        ((0, 0), (1, 1)),
        dimension_numbers=("NHWC", "HWIO", "NHWC"),
        preferred_element_type=jnp.float32,
    )


def kernel_grad(padded, cotangent):
    result = lax.conv_general_dilated(
        padded,
        cotangent,
        (1, 1),
        ((0, 0), (1, 1)),
        dimension_numbers=("CHWN", "IHWO", "HWNC"),
        preferred_element_type=jnp.float32,
    )
    return result.reshape(-1, result.shape[-1])


def project(values, weight):
    flat = values.reshape(-1, values.shape[-1])
    return jnp.dot(flat, weight, preferred_element_type=jnp.float32).reshape(
        values.shape[:-1] + (weight.shape[1],)
    )


def flipped(weight, channels):
    grid = weight.reshape(3, 3, channels, channels)[::-1, ::-1]
    return jnp.swapaxes(grid, 2, 3).reshape(9 * channels, channels)


def contract_rows(left, right):
    return lax.dot_general(
        left, right, (((0,), (0,)), ((), ())), preferred_element_type=jnp.float32
    )


def per_device(latent, hint, decoder_in, target, first_convs, second_convs, pointwise_weights):
    samples, height, width, channels = latent.shape
    first_all, point_all = (
        lax.all_gather(first_convs, "dp", axis=2, tiled=True),
        lax.all_gather(pointwise_weights, "dp", axis=2, tiled=True),
    )
    second_all = lax.all_gather(second_convs, "dp", axis=1, tiled=True)
    first_left = first_all[0, 0]
    first_right = first_all[0, 1]
    second_main = second_all[0]
    second_back = flipped(second_main, channels)
    point_left = point_all[0, 0]
    point_right = point_all[0, 1]
    right_back = point_right.T
    segment_zero = lax.axis_index("segment") == 0
    scale = 1.0 / math.sqrt(samples * lax.axis_size("dp") * height * lax.axis_size("rows") * width)
    blocks = 1
    block = samples // blocks
    plane = (block, height, width, channels)
    empty = jnp.zeros(plane, jnp.bfloat16)
    received = jnp.zeros((2,) + plane, jnp.bfloat16)
    returned = empty
    error_half = empty
    dec_grad = empty
    grad_first = jnp.zeros((9 * channels, channels), jnp.float32)
    grad_zero = jnp.zeros((channels, channels), jnp.float32)
    saved = [None] * blocks
    for tick in range(blocks + 2):
        forward_zero = tick < blocks
        decode = 1 <= tick <= blocks
        backward_zero = tick >= 2
        if forward_zero or decode:
            first_index = min(tick, blocks - 1)

            def inputs_zero():
                mixed = (latent.astype(jnp.float32) + project(hint, point_left)).astype(
                    jnp.bfloat16
                )
                return jnp.stack([latent, mixed])

            def inputs_one():
                return jnp.stack([received[0], decoder_in])

            pair = lax.cond(segment_zero, inputs_zero, inputs_one)
            padded = padded_2(pair, (("rows", 2),), 1)
            out_left = conv_rows(padded[0], first_left)
            out_right = conv_rows(padded[1], first_right)

            def middle_zero():
                return jax.nn.silu(out_right).astype(jnp.bfloat16)

            def middle_one():
                return (
                    latent.astype(jnp.float32) + out_left + received[1].astype(jnp.float32)
                ).astype(jnp.bfloat16)

            middle = lax.cond(segment_zero, middle_zero, middle_one)
            padded_mid = padded_2(middle, (("rows", 1),), 1)
            out_mid = conv_rows(padded_mid, second_main)

            def finish_zero():
                enc_act = jax.nn.silu(out_left).astype(jnp.bfloat16)
                control_out = (pair[1].astype(jnp.float32) + out_mid).astype(jnp.bfloat16)
                control_proj = project(control_out, point_right).astype(jnp.bfloat16)
                return (jnp.stack([enc_act, control_proj]), control_out, empty, empty)

            def finish_one():
                dec_pre = out_right + out_mid
                output = (
                    jax.nn.silu(dec_pre)
                    + project(decoder_in, point_left)
                    + project(middle, point_right)
                )
                error = (output - target.astype(jnp.float32)) * scale
                return (
                    jnp.zeros((2,) + plane, jnp.bfloat16),
                    empty,
                    error.astype(jnp.bfloat16),
                    (error * swish_slope(dec_pre)).astype(jnp.bfloat16),
                )

            outgoing, control_out, error_half, dec_grad = lax.cond(
                segment_zero, finish_zero, finish_one
            )
            if forward_zero:
                saved[first_index] = (padded[1], out_right, control_out)
                received = shifted(outgoing, "segment", 1)
        if decode or backward_zero:
            incoming = returned

            def start_zero():
                return project(incoming, right_back).astype(jnp.bfloat16)

            def start_one():
                return dec_grad

            back = lax.cond(segment_zero, start_zero, start_one)
            padded_back = padded_2(back, (("rows", 1),), 1)
            out_back = conv_rows(padded_back, second_back)
            if backward_zero:
                held_input, held_pre, held_out = saved[tick - 2]

                def update_zero():
                    first_grad = (out_back * swish_slope(held_pre)).astype(jnp.bfloat16)
                    new_first = grad_first + kernel_grad(held_input, first_grad)
                    new_zero = grad_zero + contract_rows(
                        held_out.reshape(-1, channels), incoming.reshape(-1, channels)
                    )
                    return (new_first, new_zero, empty)

            else:

                def update_zero():
                    return (grad_first, grad_zero, empty)

            def update_one():
                skip_grad = (out_back + project(error_half, right_back)).astype(jnp.bfloat16)
                return (grad_first, grad_zero, skip_grad)

            grad_first, grad_zero, skip_grad = lax.cond(segment_zero, update_zero, update_one)
            if decode:
                returned = shifted(skip_grad, "segment", -1)
    flat_first = grad_first.reshape(-1)
    flat_zero = grad_zero.reshape(-1)
    out_first, out_zero = (
        lax.psum_scatter(flat_first, ("segment", "dp", "rows"), scatter_dimension=0, tiled=True),
        lax.psum_scatter(flat_zero, ("segment", "dp", "rows"), scatter_dimension=0, tiled=True),
    )
    return (out_first, out_zero)


def solution(mesh):
    placed = (
        P("dp", "rows", None, None),
        P("dp", "rows", None, None),
        P("dp", "rows", None, None),
        P("dp", "rows", None, None),
        P("segment", None, "dp", None),
        P("segment", "dp", None),
        P("segment", None, "dp", None),
    )
    return jax.shard_map(
        per_device,
        mesh=mesh,
        in_specs=placed,
        out_specs=(P(("segment", "dp", "rows")), P(("segment", "dp", "rows"))),
        check_vma=False,
    )
```

profile of v0, /device:TPU:17, one launch (start us, length us, event | category | flops | bytes accessed | tf_op | source)
XLA Modules:
  0.0 553.0 jit_solution(7433316878518394187)
XLA Ops:
  7.9 1.5 copy.145
  9.5 45.9 %all_gather.9 = bf16[1,2,320,320]{3,1,0,2:T(2,128)(2,1)S(1)} all-gather(bf16[1,2,5,320]{3,1,0,2:T(2,128)(2,1)} %bitcast.208), channel_id=1, replica_groups=mesh['segment'=2,'dp'=64,'rows'=4] {'dp'}, dimensions={2}, use_global_device_ids=true | all-gather | bytes 416000 | tf_op jit(solution)/shard_map/all_gather | solution.py:78
  56.3 3.1 collective-permute-start
  59.4 1.3 collective-permute-start.1
  61.0 3.2 collective-permute-done.1
  65.7 32.6 %all-gather.3.cloned.1.call-done = bf16[1,2,2880,320]{3,1,0,2:T(2,128)(2,1)} async-done(((bf16[1,2,45,320]{3,1,0,2:T(2,128)(2,1)}), bf16[1,2,2880,320]{3,1,0,2:T(2,128)(2,1)}) %all-gather.3.cloned.1.call-update) | async-done | bytes 3686416 | tf_op jit(solution)/shard_map/all_gather | solution.py:77
  98.3 9.5 %fusion.71 = (bf16[1,1,2880,320]{3,1,0,2:T(2,128)(2,1)S(1)}, bf16[1,1,2880,320]{3,1,0,2:T(2,128)(2,1)S(1)}) fusion(bf16[1,2,2880,320]{3,1,0,2:T(2,128)(2,1)} %all-gather.3.cloned.1.call-done), kind=kLoop, calls=%fused_computation.126 | loop fusion | bytes 7372800 | tf_op jit(solution)/shard_map/slice | solution.py:81
  114.3 4.6 collective-permute-start.2
  118.9 66.2 %all-gather.5.cloned.1.call-done = bf16[1,2880,320]{2,0,1:T(2,128)(2,1)} async-done(((bf16[1,45,320]{2,0,1:T(2,128)(2,1)}), bf16[1,2880,320]{2,0,1:T(2,128)(2,1)}) %all-gather.5.cloned.1.call-update) | async-done | bytes 1843216 | tf_op jit(solution)/shard_map/all_gather | solution.py:80
  185.1 2.6 copy.189
  192.2 7.1 %collective-permute-done.4 = bf16[2,2,4,16,320]{4,3,2,1,0:T(8,128)(2,1)} collective-permute-done((bf16[2,2,4,16,320]{4,3,2,1,0:T(8,128)(2,1)S(1)}, bf16[2,2,4,16,320]{4,3,2,1,0:T(8,128)(2,1)}, u32[]{:S(2)}, u32[]{:S(2)}) %collective-permute-start.4) | collective-permute-done | bytes 163872 | tf_op jit(solution)/shard_map/ppermute | solution.py:24
  200.3 1.4 collective-permute-start.6
  201.7 4.2 collective-permute-start.5
  212.0 1.3 collective-permute-start.8
  213.3 4.3 collective-permute-start.7
  222.0 4.3 collective-permute-start.9
  229.4 4.4 collective-permute-start.11
  236.1 4.6 collective-permute-start.12
  243.5 2.4 conditional.25
  243.5 2.3 broadcast_in_dim.13
  245.9 5.7 %reshape.49 = f32[921600]{0:T(1024)} reshape(f32[2880,320]{1,0:T(8,128)} %get-tuple-element.146) | data formatting | bytes 7372800 | tf_op jit(solution)/shard_map/reshape | solution.py:196
  252.7 291.1 %all-reduce.6.cloned.1.call-done = (f32[921600]{0:T(1024)}, f32[102400]{0:T(1024)}) async-done(((f32[921600]{0:T(1024)}, f32[102400]{0:T(1024)}), (f32[921600]{0:T(1024)}, f32[102400]{0:T(1024)})) %all-reduce.6.cloned.1.call-update) | async-done | bytes 4096016
  543.8 1.4 dynamic-slice
  545.2 1.3 dynamic-slice.1
  (144 shorter events, 37.8 us)
Async XLA Ops:
  7.2 91.1 %all-gather.3.cloned.1.call-start = ((), (), s32[]{:S(2)}) async-start(), calls=%async_computation | async-start | bytes 4492800 | tf_op jit(solution)/shard_map/all_gather | solution.py:77
  7.2 48.9 %copy-start = (bf16[2,4,16,320]{3,2,1,0:T(8,128)(2,1)S(1)}, bf16[2,4,16,320]{3,2,1,0:T(8,128)(2,1)}, u32[]{:S(2)}) copy-start(bf16[2,4,16,320]{3,2,1,0:T(8,128)(2,1)} %param.27) | copy-start | bytes 245764
  7.2 48.9 %copy-start.5 = (bf16[2,4,16,320]{3,2,1,0:T(8,128)(2,1)S(1)}, bf16[2,4,16,320]{3,2,1,0:T(8,128)(2,1)}, u32[]{:S(2)}) copy-start(bf16[2,4,16,320]{3,2,1,0:T(8,128)(2,1)} %param.29) | copy-start | bytes 245764
  7.2 48.9 %copy-start.8 = (bf16[2,4,16,320]{3,2,1,0:T(8,128)(2,1)S(1)}, bf16[2,4,16,320]{3,2,1,0:T(8,128)(2,1)}, u32[]{:S(2)}) copy-start(bf16[2,4,16,320]{3,2,1,0:T(8,128)(2,1)} %param.28) | copy-start | bytes 245764
  7.9 177.2 %all-gather.5.cloned.1.call-start = ((), (), s32[]{:S(2)}) async-start(), calls=%async_computation.1 | async-start | bytes 4492800 | tf_op jit(solution)/shard_map/all_gather | solution.py:80
  9.4 534.3 %all-reduce.6.cloned.1.call-start = ((), (), s32[]{:S(2)}) async-start(), calls=%async_computation.2 | async-start | bytes 8192000
  56.3 4.5 collective-permute-start
  59.4 4.8 collective-permute-start.1
  110.0 1.4 copy-start.1
  113.0 74.7 %collective-permute-start.3 = (bf16[2,1,16,320]{3,2,1,0:T(8,128)(2,1)}, bf16[2,1,16,320]{3,2,1,0:T(8,128)(2,1)}, u32[]{:S(2)}, u32[]{:S(2)}) collective-permute-start(bf16[2,1,16,320]{3,2,1,0:T(8,128)(2,1)} %get-tuple-element.279), channel_id=1, source_target_pairs={{1,0},{2,1},{3,2},{5,4},{6,5},{7,6},{9,8},{10,9},{11,10},{13,12},{... | collective-permute-start | bytes 61448 | tf_op jit(solution)/shard_map/ppermute | solution.py:16
  114.3 73.4 %collective-permute-start.2 = (bf16[2,1,16,320]{3,2,1,0:T(8,128)(2,1)}, bf16[2,1,16,320]{3,2,1,0:T(8,128)(2,1)}, u32[]{:S(2)}, u32[]{:S(2)}) collective-permute-start(bf16[2,1,16,320]{3,2,1,0:T(8,128)(2,1)} %get-tuple-element.278), channel_id=1, source_target_pairs={{0,1},{1,2},{2,3},{4,5},{5,6},{6,7},{8,9},{9,10},{10,11},{12,13},{... | collective-permute-start | bytes 61448 | tf_op jit(solution)/shard_map/ppermute | solution.py:13
  190.0 9.3 %copy-start.6 = (bf16[2,4,16,320]{3,2,1,0:T(8,128)(2,1)S(1)}, bf16[2,4,16,320]{3,2,1,0:T(8,128)(2,1)}, u32[]{:S(2)}) copy-start(bf16[2,4,16,320]{3,2,1,0:T(8,128)(2,1)} %param.29) | copy-start | bytes 245764
  190.9 8.4 %collective-permute-start.4 = (bf16[2,2,4,16,320]{4,3,2,1,0:T(8,128)(2,1)S(1)}, bf16[2,2,4,16,320]{4,3,2,1,0:T(8,128)(2,1)}, u32[]{:S(2)}, u32[]{:S(2)}) collective-permute-start(bf16[2,2,4,16,320]{4,3,2,1,0:T(8,128)(2,1)S(1)} %get-tuple-element.142), channel_id=1, source_target_pairs={{0,256},{1,257},{2,258},{3,259},{4,260},{5,261},{6,262},{7,263},{8... | collective-permute-start | bytes 491528 | tf_op jit(solution)/shard_map/ppermute | solution.py:24
  200.2 7.5 %copy-start.4 = (bf16[1,1,2880,320]{3,2,1,0:T(8,128)(2,1)S(1)}, bf16[1,1,2880,320]{3,2,1,0:T(8,128)(2,1)}, u32[]{:S(2)}) copy-start(bf16[1,1,2880,320]{3,2,1,0:T(8,128)(2,1)} %copy-done.3) | copy-start | bytes 5529604
  200.3 5.6 %collective-permute-start.6 = (bf16[2,2,1,16,320]{4,3,2,1,0:T(8,128)(2,1)S(1)}, bf16[2,2,1,16,320]{4,3,2,1,0:T(8,128)(2,1)S(1)}, u32[]{:S(2)}, u32[]{:S(2)}) collective-permute-start(bf16[2,2,1,16,320]{4,3,2,1,0:T(8,128)(2,1)S(1)} %get-tuple-element.269), channel_id=1, source_target_pairs={{1,0},{2,1},{3,2},{5,4},{6,5},{7,6},{9,8},{10,9},{11,10},{13,12},{... | collective-permute-start | bytes 122888 | tf_op jit(solution)/shard_map/ppermute | solution.py:16
  201.7 5.2 collective-permute-start.5
  208.5 1.6 copy-start.2
  212.0 5.6 %collective-permute-start.8 = (bf16[2,1,16,320]{3,2,1,0:T(8,128)(2,1)S(1)}, bf16[2,1,16,320]{3,2,1,0:T(8,128)(2,1)S(1)}, u32[]{:S(2)}, u32[]{:S(2)}) collective-permute-start(bf16[2,1,16,320]{3,2,1,0:T(8,128)(2,1)S(1)} %get-tuple-element.277), channel_id=1, source_target_pairs={{1,0},{2,1},{3,2},{5,4},{6,5},{7,6},{9,8},{10,9},{11,10},{13,12},{... | collective-permute-start | bytes 61448 | tf_op jit(solution)/shard_map/ppermute | solution.py:16
  213.3 5.2 collective-permute-start.7
  220.7 5.6 %collective-permute-start.10 = (bf16[2,1,16,320]{3,2,1,0:T(8,128)(2,1)S(1)}, bf16[2,1,16,320]{3,2,1,0:T(8,128)(2,1)S(1)}, u32[]{:S(2)}, u32[]{:S(2)}) collective-permute-start(bf16[2,1,16,320]{3,2,1,0:T(8,128)(2,1)S(1)} %get-tuple-element.275), channel_id=1, source_target_pairs={{1,0},{2,1},{3,2},{5,4},{6,5},{7,6},{9,8},{10,9},{11,10},{13,12},{... | collective-permute-start | bytes 61448 | tf_op jit(solution)/shard_map/ppermute | solution.py:16
  222.0 5.2 collective-permute-start.9
  229.4 5.3 collective-permute-start.11
  234.8 5.9 %collective-permute-start.13 = (bf16[2,1,16,320]{3,2,1,0:T(8,128)(2,1)S(1)}, bf16[2,1,16,320]{3,2,1,0:T(8,128)(2,1)S(1)}, u32[]{:S(2)}, u32[]{:S(2)}) collective-permute-start(bf16[2,1,16,320]{3,2,1,0:T(8,128)(2,1)S(1)} %get-tuple-element.273), channel_id=1, source_target_pairs={{1,0},{2,1},{3,2},{5,4},{6,5},{7,6},{9,8},{10,9},{11,10},{13,12},{... | collective-permute-start | bytes 61448 | tf_op jit(solution)/shard_map/ppermute | solution.py:16
  236.1 5.5 collective-permute-start.12
  (5 other events, 5.1 us)
Sparse Core Ops, SparseCore 0:
  11.0 87.2 all-gather.2
  101.4 83.6 all-gather.4
  252.8 290.8 all-reduce.5
where the time goes:
time: 554 us; the launch traced here: 553 us
  waiting for transfers between devices  406 us (73%)
  blocking collectives  45.9 us (8%)
  starting transfers between devices  38.6 us (7%)
  local copies, waits for them, and re-layouts  37 us (7%)
  between operations  14.7 us (3%)
  matrix products  7.18 us (1%)
    unnamed x4, waiting for transfers between devices  292 us
    all_gather x1, waiting for transfers between devices, per_device(): second_all = lax.all_gather(second_convs, 'dp', axis=1, tiled=True)  66.2 us
    all_gather x1, blocking collectives, per_device(): lax.all_gather(pointwise_weights, 'dp', axis=2, tiled=True)  45.9 us
    all_gather x1, waiting for transfers between devices, per_device(): lax.all_gather(first_convs, 'dp', axis=2, tiled=True)  32.6 us
    ppermute x6, starting transfers between devices, padded_2(): lax.ppermute(lax.slice_in_dim(block, block.shape[dim] - width, None, axis...  25 us
  transfers between devices with their start and end apart: 17, of which 10 were waited for; matrix products, arithmetic and copies ran while one was open for 4% of the time, Pallas kernels for 0%

commit v1 on v0

--- a/solution.py
+++ b/solution.py
@@ -74,7 +74,9 @@
 def per_device(latent, hint, decoder_in, target, first_convs, second_convs, pointwise_weights):
     samples, height, width, channels = latent.shape
     first_all, point_all = (
-        lax.all_gather(first_convs, "dp", axis=2, tiled=True),
+        jnp.concatenate(
+            lax.all_to_all(jnp.stack([first_convs] * lax.axis_size("dp")), "dp", 0, 0), axis=2
+        ),
         lax.all_gather(pointwise_weights, "dp", axis=2, tiled=True),
     )
     second_all = lax.all_gather(second_convs, "dp", axis=1, tiled=True)

time: 554 us -> 606 us (1.094)
  blocking collectives: 45.9 us -> 165 us
  waiting for transfers between devices: 406 us -> 318 us
  starting transfers between devices: 38.6 us -> 53.2 us
    all_gather x1, blocking collectives: 45.9 us -> 165 us  [per_device(): lax.all_gather(pointwise_weights, 'dp', axis=2, tiled=True)]
    all_gather x1, waiting for transfers between devices: 66.2 us -> 0.01 us  [per_device(): second_all = lax.all_gather(second_convs, 'dp', axis=1, tiled=True)]
    all_gather x1 -> x0, waiting for transfers between devices: 32.6 us -> none  [per_device(): lax.all_gather(first_convs, 'dp', axis=2, tiled=True)]
    all_to_all x0 -> x1, starting transfers between devices: none -> 16.2 us  [per_device(): lax.all_to_all(jnp.stack([first_convs] * lax.axis_size('dp')), 'dp', 0, 0)]
    ppermute x2, waiting for transfers between devices: 8.03 us -> 17.1 us  [shifted(): return lax.ppermute(array, axis, pairs)]
    unnamed x4 -> x3, waiting for transfers between devices: 292 us -> 293 us
  transfers between devices with their start and end apart: 17 -> 17, of which waited for: 10 -> 8; matrix products, arithmetic and copies ran while one was open for 4% -> 3% of each run, Pallas kernels for 0% -> 0%
where the time goes in v1:
time: 606 us; the launch traced here: 604 us
  waiting for transfers between devices  318 us (52%)
  blocking collectives  165 us (27%)
  starting transfers between devices  53.2 us (9%)
  local copies, waits for them, and re-layouts  41.7 us (7%)
  between operations  15 us (2%)
  matrix products  7.18 us (1%)
    unnamed x3, waiting for transfers between devices  293 us
    all_gather x1, blocking collectives, per_device(): lax.all_gather(pointwise_weights, 'dp', axis=2, tiled=True)  165 us
    ppermute x6, starting transfers between devices, padded_2(): lax.ppermute(lax.slice_in_dim(block, block.shape[dim] - width, None, axis...  23.4 us
    ppermute x2, waiting for transfers between devices, shifted(): return lax.ppermute(array, axis, pairs)  17.1 us
    all_to_all x1, starting transfers between devices, per_device(): lax.all_to_all(jnp.stack([first_convs] * lax.axis_size('dp')), 'dp', 0, 0)  16.2 us
  transfers between devices with their start and end apart: 17, of which 8 were waited for; matrix products, arithmetic and copies ran while one was open for 3% of the time, Pallas kernels for 0%

profile of v1, /device:TPU:17, one launch (start us, length us, event | category | flops | bytes accessed | tf_op | source)
XLA Modules:
  0.0 604.4 jit_solution(11828064351746311758)
XLA Ops:
  7.2 5.3 stack.28
  12.5 16.2 %all-to-all-start = ((bf16[64,1,2,45,320]{4,2,3,1,0:T(2,128)(2,1)}), bf16[64,1,2,45,320]{4,2,3,1,0:T(2,128)(2,1)}, u32[]{:S(2)}, u32[]{:S(2)}) async-start(bf16[64,1,2,45,320]{4,2,3,1,0:T(2,128)(2,1)} %stack.28), calls=%async_computation | async-start | bytes 8847360 | tf_op jit(solution)/shard_map/all_to_all | solution.py:78
  29.6 165.4 %all_gather.6 = bf16[1,2,320,320]{3,1,0,2:T(2,128)(2,1)S(1)} all-gather(bf16[1,2,5,320]{3,1,0,2:T(2,128)(2,1)S(1)} %bitcast.211), channel_id=1, replica_groups=mesh['segment'=2,'dp'=64,'rows'=4] {'dp'}, dimensions={2}, use_global_device_ids=true | all-gather | bytes 416000 | tf_op jit(solution)/shard_map/all_gather | solution.py:80
  195.9 1.4 collective-permute-start
  197.4 1.3 collective-permute-start.1
  199.0 3.6 collective-permute-done.1
  204.1 9.5 %fusion.71 = (bf16[1,1,2880,320]{3,1,2,0:T(2,128)(2,1)S(1)}, bf16[1,1,2880,320]{3,1,2,0:T(2,128)(2,1)S(1)}) fusion(bf16[1,2,2880,320]{3,1,2,0:T(2,128)(2,1)} %bitcast.35), kind=kLoop, calls=%fused_computation.126 | loop fusion | bytes 7372800 | tf_op jit(solution)/shard_map/slice | solution.py:83
  220.1 4.6 collective-permute-start.2
  224.7 2.6 copy.229
  231.8 16.2 %collective-permute-done.4 = bf16[2,2,4,16,320]{4,3,2,1,0:T(8,128)(2,1)} collective-permute-done((bf16[2,2,4,16,320]{4,3,2,1,0:T(8,128)(2,1)S(1)}, bf16[2,2,4,16,320]{4,3,2,1,0:T(8,128)(2,1)}, u32[]{:S(2)}, u32[]{:S(2)}) %collective-permute-start.4) | collective-permute-done | bytes 163872 | tf_op jit(solution)/shard_map/ppermute | solution.py:24
  249.0 1.4 collective-permute-start.6
  250.4 4.0 collective-permute-start.5
  260.7 1.3 collective-permute-start.8
  262.0 4.3 collective-permute-start.7
  269.5 1.3 collective-permute-start.10
  270.8 4.3 collective-permute-start.9
  278.2 4.4 collective-permute-start.11
  284.8 4.8 collective-permute-start.12
  292.3 2.4 conditional.25
  292.3 2.4 broadcast_in_dim.13
  294.7 5.7 reshape.60
  301.5 293.4 %all-reduce.6.cloned.1.call-done = (f32[921600]{0:T(1024)}, f32[102400]{0:T(1024)}) async-done(((f32[921600]{0:T(1024)}, f32[102400]{0:T(1024)}), (f32[921600]{0:T(1024)}, f32[102400]{0:T(1024)})) %all-reduce.6.cloned.1.call-update) | async-done | bytes 4096016
  594.9 1.4 dynamic-slice
  596.3 1.3 dynamic-slice.1
  (152 shorter events, 36.5 us)
Async XLA Ops:
  12.5 16.3 %copy-start.12 = (bf16[1,45,320]{2,1,0:T(8,128)(2,1)S(1)}, bf16[1,45,320]{2,1,0:T(8,128)(2,1)}, u32[]{:S(2)}) copy-start(bf16[1,45,320]{2,1,0:T(8,128)(2,1)} %param.32) | copy-start | bytes 86404
  12.5 17.1 %copy-start.13 = (bf16[1,2,5,320]{3,1,2,0:T(2,128)(2,1)S(1)}, bf16[1,2,5,320]{3,1,2,0:T(2,128)(2,1)}, u32[]{:S(2)}) copy-start(bf16[1,2,5,320]{3,1,2,0:T(2,128)(2,1)} %param.33) | copy-start | bytes 19204
  12.5 191.6 %all-to-all-start = ((bf16[64,1,2,45,320]{4,2,3,1,0:T(2,128)(2,1)}), bf16[64,1,2,45,320]{4,2,3,1,0:T(2,128)(2,1)}, u32[]{:S(2)}, u32[]{:S(2)}) async-start(bf16[64,1,2,45,320]{4,2,3,1,0:T(2,128)(2,1)} %stack.28), calls=%async_computation | async-start | bytes 8847360 | tf_op jit(solution)/shard_map/all_to_all | solution.py:78
  28.7 167.1 %copy-start = (bf16[2,4,16,320]{3,2,1,0:T(8,128)(2,1)S(1)}, bf16[2,4,16,320]{3,2,1,0:T(8,128)(2,1)}, u32[]{:S(2)}) copy-start(bf16[2,4,16,320]{3,2,1,0:T(8,128)(2,1)} %param.27) | copy-start | bytes 245764
  28.7 167.1 %copy-start.5 = (bf16[2,4,16,320]{3,2,1,0:T(8,128)(2,1)S(1)}, bf16[2,4,16,320]{3,2,1,0:T(8,128)(2,1)}, u32[]{:S(2)}) copy-start(bf16[2,4,16,320]{3,2,1,0:T(8,128)(2,1)} %param.29) | copy-start | bytes 245764
  28.7 167.1 %copy-start.8 = (bf16[2,4,16,320]{3,2,1,0:T(8,128)(2,1)S(1)}, bf16[2,4,16,320]{3,2,1,0:T(8,128)(2,1)}, u32[]{:S(2)}) copy-start(bf16[2,4,16,320]{3,2,1,0:T(8,128)(2,1)} %param.28) | copy-start | bytes 245764
  28.7 196.0 %all-gather.2.cloned.1.call-start = ((), (), s32[]{:S(2)}) async-start(), calls=%async_computation.1 | async-start | bytes 4492800 | tf_op jit(solution)/shard_map/all_gather | solution.py:82
  29.5 565.4 %all-reduce.6.cloned.1.call-start = ((), (), s32[]{:S(2)}) async-start(), calls=%async_computation.2 | async-start | bytes 8192000
  195.9 2.8 collective-permute-start
  197.4 5.2 collective-permute-start.1
  218.8 8.5 %collective-permute-start.3 = (bf16[2,1,16,320]{3,2,1,0:T(8,128)(2,1)}, bf16[2,1,16,320]{3,2,1,0:T(8,128)(2,1)}, u32[]{:S(2)}, u32[]{:S(2)}) collective-permute-start(bf16[2,1,16,320]{3,2,1,0:T(8,128)(2,1)} %get-tuple-element.309), channel_id=1, source_target_pairs={{1,0},{2,1},{3,2},{5,4},{6,5},{7,6},{9,8},{10,9},{11,10},{13,12},{... | collective-permute-start | bytes 61448 | tf_op jit(solution)/shard_map/ppermute | solution.py:16
  220.1 7.3 %collective-permute-start.2 = (bf16[2,1,16,320]{3,2,1,0:T(8,128)(2,1)}, bf16[2,1,16,320]{3,2,1,0:T(8,128)(2,1)}, u32[]{:S(2)}, u32[]{:S(2)}) collective-permute-start(bf16[2,1,16,320]{3,2,1,0:T(8,128)(2,1)} %get-tuple-element.308), channel_id=1, source_target_pairs={{0,1},{1,2},{2,3},{4,5},{5,6},{6,7},{8,9},{9,10},{10,11},{12,13},{... | collective-permute-start | bytes 61448 | tf_op jit(solution)/shard_map/ppermute | solution.py:13
  229.7 18.3 %copy-start.6 = (bf16[2,4,16,320]{3,2,1,0:T(8,128)(2,1)S(1)}, bf16[2,4,16,320]{3,2,1,0:T(8,128)(2,1)}, u32[]{:S(2)}) copy-start(bf16[2,4,16,320]{3,2,1,0:T(8,128)(2,1)} %param.29) | copy-start | bytes 245764
  230.5 17.5 %collective-permute-start.4 = (bf16[2,2,4,16,320]{4,3,2,1,0:T(8,128)(2,1)S(1)}, bf16[2,2,4,16,320]{4,3,2,1,0:T(8,128)(2,1)}, u32[]{:S(2)}, u32[]{:S(2)}) collective-permute-start(bf16[2,2,4,16,320]{4,3,2,1,0:T(8,128)(2,1)S(1)} %get-tuple-element.142), channel_id=1, source_target_pairs={{0,256},{1,257},{2,258},{3,259},{4,260},{5,261},{6,262},{7,263},{8... | collective-permute-start | bytes 491528 | tf_op jit(solution)/shard_map/ppermute | solution.py:24
  249.0 7.5 %copy-start.4 = (bf16[1,1,2880,320]{3,2,1,0:T(8,128)(2,1)S(1)}, bf16[1,1,2880,320]{3,2,1,0:T(8,128)(2,1)}, u32[]{:S(2)}) copy-start(bf16[1,1,2880,320]{3,2,1,0:T(8,128)(2,1)} %copy-done.3) | copy-start | bytes 5529604
  249.0 5.4 collective-permute-start.6
  250.4 5.2 collective-permute-start.5
  260.7 5.6 collective-permute-start.8
  262.0 5.2 collective-permute-start.7
  269.5 5.6 collective-permute-start.10
  270.8 5.2 collective-permute-start.9
  278.2 5.3 collective-permute-start.11
  283.5 6.1 %collective-permute-start.13 = (bf16[2,1,16,320]{3,2,1,0:T(8,128)(2,1)S(1)}, bf16[2,1,16,320]{3,2,1,0:T(8,128)(2,1)S(1)}, u32[]{:S(2)}, u32[]{:S(2)}) collective-permute-start(bf16[2,1,16,320]{3,2,1,0:T(8,128)(2,1)S(1)} %get-tuple-element.303), channel_id=1, source_target_pairs={{1,0},{2,1},{3,2},{5,4},{6,5},{7,6},{9,8},{10,9},{11,10},{13,12},{... | collective-permute-start | bytes 61448 | tf_op jit(solution)/shard_map/ppermute | solution.py:16
  284.8 5.5 collective-permute-start.12
  (9 other events, 15.9 us)
Sparse Core Ops, SparseCore 0:
  32.6 179.1 all-gather.1
  301.6 293.2 all-reduce.5
